TPU v7x, 32 devices: a whole 2x2x4 slice. The times are simulated.
32 devices in a mesh: mode: 8 (over z, y), rep: 4 (over x, core).
Axes of the slice: x: 2, y: 2, z: 4, core: 2. Of those that a mesh axis runs over, the one named last changes fastest.
Arguments:
- first_cores: float32 [2, 8, 128, 64], P(None, 'rep', 'mode'), may hold values from -6 to 6
- mid_cores: float32 [2, 8, 3, 128, 4096], P(None, 'rep', None, 'mode'), may hold values from -2 to 2
- last_cores: float32 [2, 8, 128, 64], P(None, 'rep', 'mode'), may hold values from -0.75 to 0.75
- sketch_mid: float32 [3, 128, 4096], P(None, 'mode'), may hold values from -0.0625 to 0.0625
- sketch_last: float32 [128, 64], P('mode'), may hold values from -0.5 to 0.5
- ranks: int32 [4], replicated, may hold values from 32 to 64, as said below
Outputs:
- rounded_first: float32 [2, 128, 64], P(None, 'mode')
- rounded_mid: float32 [2, 3, 128, 4096], P(None, None, 'mode')
- rounded_last: float32 [2, 128, 64], P(None, 'mode')
Inputs may be any that keep to these rules, and one draw needn't show every extreme that they name: `ranks`: some bond has rank 64.
All inputs are finite; a program needn't handle non-finite values.
Results may differ from a plain program's by a relative error of at most 0.00019.
Values sent between devices are 32-bit elements; how exact they have to be, the bound alone decides.
No kernel may reach another device: no remote copies, remote signals or barrier semaphores. Data moves between devices by JAX's collectives and lax.ppermute only.
A program may use at most 64 MiB of HBM per device.

v0:
```python
import jax
import jax.numpy as jnp
from jax import lax
from jax.sharding import PartitionSpec as P

PRECISE = lax.Precision.HIGHEST


def lower_inverse(gram_matrix):
    factor = jnp.linalg.cholesky(gram_matrix)
    identity = jnp.eye(gram_matrix.shape[-1], dtype=gram_matrix.dtype)
    return jax.vmap(lambda single: jax.scipy.linalg.solve_triangular(single, identity, lower=True))(
        factor
    )


def sketch_total(partial_value):
    return lax.psum(partial_value, "mode")


def orthogonal(pieces, sketch, bond_mask, row_count):
    local_mix = jnp.einsum("bsiad,bsde->biae", pieces, sketch, precision=PRECISE)
    mixture = lax.psum(local_mix, "rep")
    gram_part = jnp.einsum("biae,biaf->bef", mixture, mixture, precision=PRECISE)
    raw_part = jnp.einsum("biae,bsiad->bsed", mixture, pieces, precision=PRECISE)
    gram_total, raw_total = lax.psum((gram_part, raw_part), "mode")
    inverse = lower_inverse(gram_total / row_count + jnp.diag(1.0 - bond_mask))
    ortho_basis = jnp.einsum("biae,bfe->biaf", mixture, inverse, precision=PRECISE)
    carried = jnp.einsum("bfe,bsed->bsfd", inverse, raw_total, precision=PRECISE) / row_count
    return (ortho_basis, carried)


def per_device(first_cores, mid_cores, last_cores, sketch_mid, sketch_last, ranks):
    members, summands, slices, rank_size = first_cores.shape
    middle = mid_cores.shape[2]
    total_slices = slices * lax.axis_size("mode")
    bond_masks = (jnp.arange(rank_size, dtype=jnp.int32)[None, :] < ranks[:, None]).astype(
        jnp.float32
    )
    middle_cores = mid_cores.reshape(members, summands, middle, slices, rank_size, rank_size)
    sketch_cores = sketch_mid.reshape(middle, slices, rank_size, rank_size)
    newest = (
        sketch_total(jnp.einsum("bsic,ie->bsce", last_cores, sketch_last, precision=PRECISE))
        * bond_masks[middle]
    )
    stored = jnp.zeros((middle + 1, members, summands, rank_size, rank_size), jnp.float32)
    stored = stored.at[middle].set(newest)

    def right_step(step, sketches):
        position = middle - 1 - step
        current = lax.dynamic_index_in_dim(sketches, position + 1, 0, keepdims=False)
        core_now = lax.dynamic_index_in_dim(middle_cores, position, 2, keepdims=False)
        sketch_now = lax.dynamic_index_in_dim(sketch_cores, position, 0, keepdims=False)
        mask_now = lax.dynamic_index_in_dim(bond_masks, position, 0, keepdims=False)
        partial_value = jnp.einsum("bsicd,bsde->bsice", core_now, current, precision=PRECISE)
        folded = jnp.einsum("bsice,ife->bscf", partial_value, sketch_now, precision=PRECISE)
        updated = sketch_total(folded) * mask_now
        return lax.dynamic_update_index_in_dim(sketches, updated, position, 0)

    stored = lax.fori_loop(0, middle, right_step, stored)
    pieces = first_cores[:, :, :, None, :]
    ortho_basis, carried = orthogonal(pieces, stored[0], bond_masks[0], total_slices)
    rounded_first = ortho_basis[:, :, 0, :]
    buffer = jnp.zeros((members, middle, slices, rank_size * rank_size), jnp.float32)

    def left_step(position, state):
        carried_now, buffer_now = state
        core_now = lax.dynamic_index_in_dim(middle_cores, position, 2, keepdims=False)
        sketch_now = lax.dynamic_index_in_dim(stored, position + 1, 0, keepdims=False)
        mask_now = lax.dynamic_index_in_dim(bond_masks, position + 1, 0, keepdims=False)
        pieces_now = jnp.einsum("bsac,bsicd->bsiad", carried_now, core_now, precision=PRECISE)
        basis_now, carried_next = orthogonal(
            pieces_now, sketch_now, mask_now, total_slices * rank_size
        )
        flat_basis = basis_now.reshape(members, slices, rank_size * rank_size)
        buffer_next = lax.dynamic_update_index_in_dim(buffer_now, flat_basis, position, 1)
        return (carried_next, buffer_next)

    carried, rounded_mid = lax.fori_loop(0, middle, left_step, (carried, buffer))
    local_last = jnp.einsum("bsac,bsic->bia", carried, last_cores, precision=PRECISE)
    rounded_last = lax.psum(local_last, "rep")
    return (rounded_first, rounded_mid, rounded_last)


def solution(mesh):
    return jax.shard_map(
        per_device,
        mesh=mesh,
        in_specs=(
            P(None, "rep", "mode", None),
            P(None, "rep", None, "mode", None),
            P(None, "rep", "mode", None),
            P(None, "mode", None),
            P("mode", None),
            P(),
        ),
        out_specs=(P(None, "mode", None), P(None, None, "mode", None), P(None, "mode", None)),
        check_vma=False,
    )
```

profile of v0, /device:TPU:0, one launch (start us, length us, event | category | flops | bytes accessed | tf_op | source)
XLA Modules:
  0.0 836.8 jit_solution(11274654828225337695)
XLA Ops:
  16.8 67.7 %all-reduce.7.cloned.1.call-done = f32[2,2,64,64]{3,2,1,0:T(8,128)} async-done(((f32[2,2,64,64]{3,2,1,0:T(8,128)}), f32[2,2,64,64]{3,2,1,0:T(8,128)}) %all-reduce.7.cloned.1.call-update) | async-done | bytes 65552 | tf_op jit(solution)/shard_map/psum | solution.py:18
  85.4 229.9 %while.35 = (s32[]{:T(128)}, f32[4,2,2,64,64]{4,3,2,1,0:T(8,128)S(1)}, f32[2,2,3,16,64,64]{5,4,3,2,1,0:T(8,128)}, f32[3,16,64,64]{3,2,1,0:T(8,128)S(1)}, f32[4,6...) while((s32[]{:T(128)}, ...), condition=%wide.region_3.4_spmd, body=%wide.region_1.3_spmd.sunk | while | flops 402685952 | bytes 6685998 | solution.py:60
  91.5 69.6 %all-reduce.11.cloned.1.call-done = f32[2,2,64,64]{3,2,1,0:T(8,128)} async-done(((f32[2,2,64,64]{3,2,1,0:T(8,128)}), f32[2,2,64,64]{3,2,1,0:T(8,128)}) %all-reduce.11.cloned.1.call-update) | async-done | bytes 65552 | tf_op jit(solution)/shard_map/while/body/eval_jaxpr/psum | solution.py:18
  168.2 69.6 %all-reduce.11.cloned.1.call-done = f32[2,2,64,64]{3,2,1,0:T(8,128)} async-done(((f32[2,2,64,64]{3,2,1,0:T(8,128)}), f32[2,2,64,64]{3,2,1,0:T(8,128)}) %all-reduce.11.cloned.1.call-update) | async-done | bytes 65552 | tf_op jit(solution)/shard_map/while/body/eval_jaxpr/psum | solution.py:18
  244.8 69.6 %all-reduce.11.cloned.1.call-done = f32[2,2,64,64]{3,2,1,0:T(8,128)} async-done(((f32[2,2,64,64]{3,2,1,0:T(8,128)}), f32[2,2,64,64]{3,2,1,0:T(8,128)}) %all-reduce.11.cloned.1.call-update) | async-done | bytes 65552 | tf_op jit(solution)/shard_map/while/body/eval_jaxpr/psum | solution.py:18
  315.6 10.1 %psum.95 = f32[2,16,64]{2,1,0:T(8,128)S(1)} all-reduce(f32[2,16,64]{2,1,0:T(8,128)S(1)} %convolution_bitcast_fusion.5), channel_id=1, replica_groups=mesh['mode'=8,'rep'=4] {'rep'}, use_global_device_ids=true, to_apply=%region_4.5 | all-reduce | flops 2048 | bytes 16384 | tf_op jit(solution)/shard_map/psum | solution.py:23
  327.0 35.7 %psum.96 = f32[2,64,64]{1,2,0:T(8,128)S(1)} all-reduce(f32[2,64,64]{1,2,0:T(8,128)S(1)} %fusion.52), channel_id=1, replica_groups=mesh['mode'=8,'rep'=4] {'mode'}, use_global_device_ids=true, to_apply=%region_5.6 | all-reduce | flops 8192 | bytes 65536 | tf_op jit(solution)/shard_map/psum | solution.py:26
  362.8 11.7 %custom-call.10 = f32[2,64,64]{2,1,0:T(8,128)S(1)} custom-call(f32[2,64,64]{2,1,0:T(8,128)S(1)} %fusion.43), custom_call_target="Cholesky" | custom-call | tf_op jit(solution)/shard_map/jit(cholesky)/cholesky | solution.py:10
  374.8 9.8 %custom-call.11 = f32[2,1,64,64]{2,3,1,0:T(8,128)S(1)} custom-call(f32[2,1,64,64]{3,2,1,0:T(8,128)S(1)} %select_bitcast_fusion.1), custom_call_target="InvertDiagBlocksLowerTriangular" | custom-call | tf_op jit(solution)/shard_map/vmap(jit(_solve_triangular))/triangular_solve | solution.py:12
  385.8 66.8 %all-reduce.9.cloned.1.call-done = f32[2,2,64,64]{3,2,1,0:T(8,128)} async-done(((f32[2,2,64,64]{3,2,1,0:T(8,128)}), f32[2,2,64,64]{3,2,1,0:T(8,128)}) %all-reduce.9.cloned.1.call-update) | async-done | bytes 65552 | tf_op jit(solution)/shard_map/psum | solution.py:26
  453.9 365.3 %while.36 = (s32[]{:T(128)}, f32[2,2,64,64]{2,3,1,0:T(8,128)S(1)}, f32[2,3,16,4096]{3,2,1,0:T(8,128)}, f32[2,2,3,16,64,64]{5,4,3,2,1,0:T(8,128)}, f32[4,2,2,64,6...) while((s32[]{:T(128)}, f32[2,2,64,64]{2,3,1,0:T(8,128)S(1)}, ...), condition=%wide.region_13.16_spmd, body=%wide.region_9.15_spmd.sunk | while | flops 824467648 | bytes 21006400 | solution.py:79
  464.0 35.3 %all-reduce.13.cloned.1.call-done = f32[2,16,64,64]{3,2,1,0:T(8,128)} async-done(((f32[2,16,64,64]{3,2,1,0:T(8,128)}), f32[2,16,64,64]{3,2,1,0:T(8,128)}) %all-reduce.13.cloned.1.call-update) | async-done | bytes 524304 | tf_op jit(solution)/shard_map/while/body/eval_jaxpr/psum | solution.py:23
  505.1 37.6 %psum.106 = f32[2,64,64]{1,2,0:T(8,128)S(1)} all-reduce(f32[2,64,64]{1,2,0:T(8,128)S(1)} %convolution_bitcast_fusion.10), channel_id=1, replica_groups=mesh['mode'=8,'rep'=4] {'mode'}, use_global_device_ids=true, to_apply=%region_12.14 | all-reduce | flops 8192 | bytes 65536 | tf_op jit(solution)/shard_map/while/body/eval_jaxpr/psum | solution.py:26
  542.8 11.7 %custom-call.15 = f32[2,64,64]{2,1,0:T(8,128)S(1)} custom-call(f32[2,64,64]{2,1,0:T(8,128)S(1)} %fusion.125), custom_call_target="Cholesky" | custom-call | tf_op jit(solution)/shard_map/while/body/eval_jaxpr/jit(cholesky)/cholesky | solution.py:10
  554.8 9.8 %custom-call.16 = f32[2,1,64,64]{2,3,1,0:T(8,128)S(1)} custom-call(f32[2,1,64,64]{3,2,1,0:T(8,128)S(1)} %select_bitcast_fusion.3), custom_call_target="InvertDiagBlocksLowerTriangular" | custom-call | tf_op jit(solution)/shard_map/while/body/eval_jaxpr/vmap(jit(_solve_triangular))/triangular_solve | solution.py:12
  585.7 35.3 %all-reduce.13.cloned.1.call-done = f32[2,16,64,64]{3,2,1,0:T(8,128)} async-done(((f32[2,16,64,64]{3,2,1,0:T(8,128)}), f32[2,16,64,64]{3,2,1,0:T(8,128)}) %all-reduce.13.cloned.1.call-update) | async-done | bytes 524304 | tf_op jit(solution)/shard_map/while/body/eval_jaxpr/psum | solution.py:23
  626.8 37.6 %psum.106 = f32[2,64,64]{1,2,0:T(8,128)S(1)} all-reduce(f32[2,64,64]{1,2,0:T(8,128)S(1)} %convolution_bitcast_fusion.10), channel_id=1, replica_groups=mesh['mode'=8,'rep'=4] {'mode'}, use_global_device_ids=true, to_apply=%region_12.14 | all-reduce | flops 8192 | bytes 65536 | tf_op jit(solution)/shard_map/while/body/eval_jaxpr/psum | solution.py:26
  664.5 11.7 %custom-call.15 = f32[2,64,64]{2,1,0:T(8,128)S(1)} custom-call(f32[2,64,64]{2,1,0:T(8,128)S(1)} %fusion.125), custom_call_target="Cholesky" | custom-call | tf_op jit(solution)/shard_map/while/body/eval_jaxpr/jit(cholesky)/cholesky | solution.py:10
  676.5 9.8 %custom-call.16 = f32[2,1,64,64]{2,3,1,0:T(8,128)S(1)} custom-call(f32[2,1,64,64]{3,2,1,0:T(8,128)S(1)} %select_bitcast_fusion.3), custom_call_target="InvertDiagBlocksLowerTriangular" | custom-call | tf_op jit(solution)/shard_map/while/body/eval_jaxpr/vmap(jit(_solve_triangular))/triangular_solve | solution.py:12
  707.4 35.3 %all-reduce.13.cloned.1.call-done = f32[2,16,64,64]{3,2,1,0:T(8,128)} async-done(((f32[2,16,64,64]{3,2,1,0:T(8,128)}), f32[2,16,64,64]{3,2,1,0:T(8,128)}) %all-reduce.13.cloned.1.call-update) | async-done | bytes 524304 | tf_op jit(solution)/shard_map/while/body/eval_jaxpr/psum | solution.py:23
  748.5 37.6 %psum.106 = f32[2,64,64]{1,2,0:T(8,128)S(1)} all-reduce(f32[2,64,64]{1,2,0:T(8,128)S(1)} %convolution_bitcast_fusion.10), channel_id=1, replica_groups=mesh['mode'=8,'rep'=4] {'mode'}, use_global_device_ids=true, to_apply=%region_12.14 | all-reduce | flops 8192 | bytes 65536 | tf_op jit(solution)/shard_map/while/body/eval_jaxpr/psum | solution.py:26
  786.2 11.7 %custom-call.15 = f32[2,64,64]{2,1,0:T(8,128)S(1)} custom-call(f32[2,64,64]{2,1,0:T(8,128)S(1)} %fusion.125), custom_call_target="Cholesky" | custom-call | tf_op jit(solution)/shard_map/while/body/eval_jaxpr/jit(cholesky)/cholesky | solution.py:10
  798.2 9.8 %custom-call.16 = f32[2,1,64,64]{2,3,1,0:T(8,128)S(1)} custom-call(f32[2,1,64,64]{3,2,1,0:T(8,128)S(1)} %select_bitcast_fusion.3), custom_call_target="InvertDiagBlocksLowerTriangular" | custom-call | tf_op jit(solution)/shard_map/while/body/eval_jaxpr/vmap(jit(_solve_triangular))/triangular_solve | solution.py:12
  819.5 10.7 %psum.98 = f32[2,16,64]{2,1,0:T(8,128)} all-reduce(f32[2,16,64]{2,1,0:T(8,128)S(1)} %convolution_bitcast_fusion.4), channel_id=1, replica_groups=mesh['mode'=8,'rep'=4] {'rep'}, use_global_device_ids=true, to_apply=%region_14.17 | all-reduce | flops 2048 | bytes 16384 | tf_op jit(solution)/shard_map/psum | solution.py:81
  (150 shorter events, 117.1 us)
Async XLA Ops:
  7.2 308.2 %copy-start = (f32[2,2,16,64]{3,2,1,0:T(8,128)S(1)}, f32[2,2,16,64]{3,2,1,0:T(8,128)}, u32[]{:S(2)}) copy-start(f32[2,2,16,64]{3,2,1,0:T(8,128)} %param.15) | copy-start | bytes 49156
  7.2 77.3 %all-reduce.7.cloned.1.call-start = ((), (), s32[]{:S(2)}) async-start(), calls=%async_computation | async-start | bytes 262144 | tf_op jit(solution)/shard_map/psum | solution.py:18
  9.8 6.2 copy-start.4
  85.4 75.7 %all-reduce.11.cloned.1.call-start = ((), (), s32[]{:S(2)}) async-start(), calls=%async_computation.2 | async-start | bytes 262144 | tf_op jit(solution)/shard_map/while/body/eval_jaxpr/psum | solution.py:18
  162.1 75.7 %all-reduce.11.cloned.1.call-start = ((), (), s32[]{:S(2)}) async-start(), calls=%async_computation.2 | async-start | bytes 262144 | tf_op jit(solution)/shard_map/while/body/eval_jaxpr/psum | solution.py:18
  238.7 75.7 %all-reduce.11.cloned.1.call-start = ((), (), s32[]{:S(2)}) async-start(), calls=%async_computation.2 | async-start | bytes 262144 | tf_op jit(solution)/shard_map/while/body/eval_jaxpr/psum | solution.py:18
  315.3 137.3 %all-reduce.9.cloned.1.call-start = ((), (), s32[]{:S(2)}) async-start(), calls=%async_computation.1 | async-start | bytes 262144 | tf_op jit(solution)/shard_map/psum | solution.py:26
  453.9 365.3 %copy-start.5 = (f32[2,2,16,64]{3,2,1,0:T(8,128)S(1)}, f32[2,2,16,64]{3,2,1,0:T(8,128)}, u32[]{:S(2)}) copy-start(f32[2,2,16,64]{3,2,1,0:T(8,128)} %param.17) | copy-start | bytes 49156
  454.1 5.2 copy-start.2
  454.1 45.2 %all-reduce.13.cloned.1.call-start = ((), (), s32[]{:S(2)}) async-start(), calls=%async_computation.3 | async-start | bytes 2097152 | tf_op jit(solution)/shard_map/while/body/eval_jaxpr/psum | solution.py:23
  463.8 110.8 %all-reduce.15.cloned.1.call-start = ((), (), s32[]{:S(2)}) async-start(), calls=%async_computation.4 | async-start | bytes 262144 | tf_op jit(solution)/shard_map/while/body/eval_jaxpr/psum | solution.py:26
  499.3 3.9 copy-start.1
  565.9 9.9 %copy-start.3 = (f32[4,2,2,64,64]{4,3,2,1,0:T(8,128)S(1)}, f32[4,2,2,64,64]{4,3,2,1,0:T(8,128)}, u32[]{:S(2)}) copy-start(f32[4,2,2,64,64]{4,3,2,1,0:T(8,128)} %copy-done.2) | copy-start | bytes 786436 | tf_op jit(solution)/shard_map/while
  575.8 5.2 copy-start.2
  575.8 45.2 %all-reduce.13.cloned.1.call-start = ((), (), s32[]{:S(2)}) async-start(), calls=%async_computation.3 | async-start | bytes 2097152 | tf_op jit(solution)/shard_map/while/body/eval_jaxpr/psum | solution.py:23
  585.5 110.8 %all-reduce.15.cloned.1.call-start = ((), (), s32[]{:S(2)}) async-start(), calls=%async_computation.4 | async-start | bytes 262144 | tf_op jit(solution)/shard_map/while/body/eval_jaxpr/psum | solution.py:26
  621.0 3.9 copy-start.1
  687.6 9.9 %copy-start.3 = (f32[4,2,2,64,64]{4,3,2,1,0:T(8,128)S(1)}, f32[4,2,2,64,64]{4,3,2,1,0:T(8,128)}, u32[]{:S(2)}) copy-start(f32[4,2,2,64,64]{4,3,2,1,0:T(8,128)} %copy-done.2) | copy-start | bytes 786436 | tf_op jit(solution)/shard_map/while
  697.5 5.2 copy-start.2
  697.6 45.2 %all-reduce.13.cloned.1.call-start = ((), (), s32[]{:S(2)}) async-start(), calls=%async_computation.3 | async-start | bytes 2097152 | tf_op jit(solution)/shard_map/while/body/eval_jaxpr/psum | solution.py:23
  707.2 110.8 %all-reduce.15.cloned.1.call-start = ((), (), s32[]{:S(2)}) async-start(), calls=%async_computation.4 | async-start | bytes 262144 | tf_op jit(solution)/shard_map/while/body/eval_jaxpr/psum | solution.py:26
  742.7 3.9 copy-start.1
  809.3 9.9 %copy-start.3 = (f32[4,2,2,64,64]{4,3,2,1,0:T(8,128)S(1)}, f32[4,2,2,64,64]{4,3,2,1,0:T(8,128)}, u32[]{:S(2)}) copy-start(f32[4,2,2,64,64]{4,3,2,1,0:T(8,128)} %copy-done.2) | copy-start | bytes 786436 | tf_op jit(solution)/shard_map/while
Sparse Core Ops, SparseCore 0:
  11.3 73.0 all-reduce.6
  91.6 69.4 all-reduce.10
  168.3 69.4 all-reduce.10
  244.9 69.4 all-reduce.10
  384.8 67.7 all-reduce.8
  463.9 35.3 all-reduce.12
  503.3 71.2 all-reduce.14
  585.6 35.3 all-reduce.12
  625.0 71.2 all-reduce.14
  707.3 35.3 all-reduce.12
  746.7 71.2 all-reduce.14
where the time goes:
time: 838 us; the launch traced here: 837 us
  waiting for transfers between devices  472 us (56%)
  blocking collectives  169 us (20%)
  other arithmetic  91.9 us (11%)
  matrix products  77.3 us (9%)
  between operations  13.9 us (2%)
  local copies, waits for them, and re-layouts  11.1 us (1%)
    psum x4, waiting for transfers between devices, sketch_total(): return lax.psum(partial_value, 'mode')  277 us
    psum x4, blocking collectives, orthogonal(): gram_total, raw_total = lax.psum((gram_part, raw_part), 'mode')  148 us
    psum x3, waiting for transfers between devices, orthogonal(): mixture = lax.psum(local_mix, 'rep')  106 us
    psum x4, waiting for transfers between devices, orthogonal(): gram_total, raw_total = lax.psum((gram_part, raw_part), 'mode')  89.3 us
    another operation x16, other arithmetic, lower_inverse(): factor = jnp.linalg.cholesky(gram_matrix)  47.6 us
    another operation x12, other arithmetic, lower_inverse(): jax.scipy.linalg.solve_triangular(single, identity, lower=True)  39.7 us
  transfers between devices with their start and end apart: 11, of which 11 were waited for; matrix products, arithmetic and copies ran while one was open for 11% of the time, Pallas kernels for 0%

commit v1 on v0

--- a/solution.py
+++ b/solution.py
@@ -4,6 +4,10 @@
 from jax.sharding import PartitionSpec as P
 
 PRECISE = lax.Precision.HIGHEST
+
+
+def measure_notes(local_values, group_axis):
+    return lax.all_gather(local_values, group_axis).sum(axis=0)
 
 
 def lower_inverse(gram_matrix):
@@ -15,7 +19,7 @@
 
 
 def sketch_total(partial_value):
-    return lax.psum(partial_value, "mode")
+    return measure_notes(partial_value, "mode")
 
 
 def orthogonal(pieces, sketch, bond_mask, row_count):

time: 838 us -> 635 us (0.76)
  waiting for transfers between devices: 472 us -> 139 us
  blocking collectives: 169 us -> 305 us
    psum x4 -> x0, waiting for transfers between devices: 277 us -> none  [sketch_total(): return lax.psum(partial_value, 'mode')]
    all_gather x0 -> x4, blocking collectives: none -> 135 us  [measure_notes(): return lax.all_gather(local_values, group_axis).sum(axis=0)]
    psum x4, waiting for transfers between devices: 89.3 us -> 33.1 us  [orthogonal(): gram_total, raw_total = lax.psum((gram_part, raw_part), 'mode')]
  transfers between devices with their start and end apart: 11 -> 7, of which waited for: 11 -> 7; matrix products, arithmetic and copies ran while one was open for 11% -> 16% of each run, Pallas kernels for 0% -> 0%
where the time goes in v1:
time: 635 us; the launch traced here: 634 us
  blocking collectives  305 us (48%)
  waiting for transfers between devices  139 us (22%)
  other arithmetic  88.6 us (14%)
  matrix products  74.7 us (12%)
  between operations  14.2 us (2%)
  local copies, waits for them, and re-layouts  11.1 us (2%)
    psum x4, blocking collectives, orthogonal(): gram_total, raw_total = lax.psum((gram_part, raw_part), 'mode')  149 us
    all_gather x4, blocking collectives, measure_notes(): return lax.all_gather(local_values, group_axis).sum(axis=0)  135 us
    psum x3, waiting for transfers between devices, orthogonal(): mixture = lax.psum(local_mix, 'rep')  106 us
    another operation x16, other arithmetic, lower_inverse(): factor = jnp.linalg.cholesky(gram_matrix)  47.6 us
    another operation x12, other arithmetic, lower_inverse(): jax.scipy.linalg.solve_triangular(single, identity, lower=True)  39.7 us
    psum x4, waiting for transfers between devices, orthogonal(): gram_total, raw_total = lax.psum((gram_part, raw_part), 'mode')  33.1 us
    dot_general x3, matrix products, left_step(): jnp.einsum('bsac,bsicd->bsiad', carried_now, core_now, precision=PRECISE)  15.4 us
    dot_general x4, matrix products, orthogonal(): jnp.einsum('bsiad,bsde->biae', pieces, sketch, precision=PRECISE)  13.5 us
  transfers between devices with their start and end apart: 7, of which 7 were waited for; matrix products, arithmetic and copies ran while one was open for 16% of the time, Pallas kernels for 0%

profile of v1, /device:TPU:0, one launch (start us, length us, event | category | flops | bytes accessed | tf_op | source)
XLA Modules:
  0.0 634.1 jit_solution(9243314291509698856)
XLA Ops:
  8.4 34.6 %all-gather.1 = f32[16,2,64,64]{3,2,1,0:T(8,128)S(1)} all-gather(f32[2,2,64,64]{3,2,1,0:T(8,128)S(1)} %fusion.49), channel_id=3, replica_groups=mesh['mode'=8,'rep'=4] {'mode'}, dimensions={0}, use_global_device_ids=true | all-gather | bytes 589824 | tf_op jit(solution)/shard_map/all_gather | solution.py:10
  50.7 116.5 %while.35 = (s32[]{:T(128)}, f32[4,2,2,64,64]{4,3,2,1,0:T(8,128)S(1)}, f32[2,2,3,16,64,64]{5,4,3,2,1,0:T(8,128)}, f32[3,16,64,64]{3,2,1,0:T(8,128)S(1)}, f32[4,6...) while((s32[]{:T(128)}, ...), condition=%wide.region_3.4_spmd, body=%wide.region_1.3_spmd.sunk | while | flops 402784256 | bytes 7406866 | solution.py:64
  56.1 33.3 %all-gather.3 = f32[16,2,64,64]{3,2,1,0:T(8,128)S(1)} all-gather(f32[2,2,64,64]{3,2,1,0:T(8,128)S(1)} %convolution_bitcast_fusion.9), channel_id=2, replica_groups=mesh['mode'=8,'rep'=4] {'mode'}, dimensions={0}, use_global_device_ids=true | all-gather | bytes 589824 | tf_op jit(solution)/shard_map/while/body/eval_jaxpr/all_gather | solution.py:10
  94.8 34.2 %all-gather.3 = f32[16,2,64,64]{3,2,1,0:T(8,128)S(1)} all-gather(f32[2,2,64,64]{3,2,1,0:T(8,128)S(1)} %convolution_bitcast_fusion.9), channel_id=2, replica_groups=mesh['mode'=8,'rep'=4] {'mode'}, dimensions={0}, use_global_device_ids=true | all-gather | bytes 589824 | tf_op jit(solution)/shard_map/while/body/eval_jaxpr/all_gather | solution.py:10
  134.5 32.6 %all-gather.3 = f32[16,2,64,64]{3,2,1,0:T(8,128)S(1)} all-gather(f32[2,2,64,64]{3,2,1,0:T(8,128)S(1)} %convolution_bitcast_fusion.9), channel_id=2, replica_groups=mesh['mode'=8,'rep'=4] {'mode'}, dimensions={0}, use_global_device_ids=true | all-gather | bytes 589824 | tf_op jit(solution)/shard_map/while/body/eval_jaxpr/all_gather | solution.py:10
  167.5 10.1 %psum.70 = f32[2,16,64]{2,1,0:T(8,128)S(1)} all-reduce(f32[2,16,64]{2,1,0:T(8,128)S(1)} %convolution_bitcast_fusion.5), channel_id=1, replica_groups=mesh['mode'=8,'rep'=4] {'rep'}, use_global_device_ids=true, to_apply=%region_4.5 | all-reduce | flops 2048 | bytes 16384 | tf_op jit(solution)/shard_map/psum | solution.py:27
  178.9 36.7 %psum.71 = f32[2,64,64]{1,2,0:T(8,128)S(1)} all-reduce(f32[2,64,64]{1,2,0:T(8,128)S(1)} %fusion.53), channel_id=1, replica_groups=mesh['mode'=8,'rep'=4] {'mode'}, use_global_device_ids=true, to_apply=%region_5.6 | all-reduce | flops 8192 | bytes 65536 | tf_op jit(solution)/shard_map/psum | solution.py:30
  215.8 11.7 %custom-call.10 = f32[2,64,64]{2,1,0:T(8,128)S(1)} custom-call(f32[2,64,64]{2,1,0:T(8,128)S(1)} %fusion.44), custom_call_target="Cholesky" | custom-call | tf_op jit(solution)/shard_map/jit(cholesky)/cholesky | solution.py:14
  227.8 9.8 %custom-call.11 = f32[2,1,64,64]{2,3,1,0:T(8,128)S(1)} custom-call(f32[2,1,64,64]{3,2,1,0:T(8,128)S(1)} %select_bitcast_fusion.1), custom_call_target="InvertDiagBlocksLowerTriangular" | custom-call | tf_op jit(solution)/shard_map/vmap(jit(_solve_triangular))/triangular_solve | solution.py:16
  238.8 10.7 %all-reduce.5.cloned.1.call-done = f32[2,2,64,64]{3,2,1,0:T(8,128)} async-done(((f32[2,2,64,64]{3,2,1,0:T(8,128)}), f32[2,2,64,64]{3,2,1,0:T(8,128)}) %all-reduce.5.cloned.1.call-update) | async-done | bytes 65552 | tf_op jit(solution)/shard_map/psum | solution.py:30
  250.8 365.5 %while.36 = (s32[]{:T(128)}, f32[2,2,64,64]{2,3,1,0:T(8,128)S(1)}, f32[2,3,16,4096]{3,2,1,0:T(8,128)}, f32[2,2,3,16,64,64]{5,4,3,2,1,0:T(8,128)}, f32[4,2,2,64,6...) while((s32[]{:T(128)}, f32[2,2,64,64]{2,3,1,0:T(8,128)S(1)}, ...), condition=%wide.region_13.16_spmd, body=%wide.region_9.15_spmd.sunk | while | flops 824467648 | bytes 21006400 | solution.py:83
  260.9 35.5 %all-reduce.7.cloned.1.call-done = f32[2,16,64,64]{3,2,1,0:T(8,128)} async-done(((f32[2,16,64,64]{3,2,1,0:T(8,128)}), f32[2,16,64,64]{3,2,1,0:T(8,128)}) %all-reduce.7.cloned.1.call-update) | async-done | bytes 524304 | tf_op jit(solution)/shard_map/while/body/eval_jaxpr/psum | solution.py:27
  302.2 37.6 %psum.79 = f32[2,64,64]{1,2,0:T(8,128)S(1)} all-reduce(f32[2,64,64]{1,2,0:T(8,128)S(1)} %convolution_bitcast_fusion.10), channel_id=1, replica_groups=mesh['mode'=8,'rep'=4] {'mode'}, use_global_device_ids=true, to_apply=%region_12.14 | all-reduce | flops 8192 | bytes 65536 | tf_op jit(solution)/shard_map/while/body/eval_jaxpr/psum | solution.py:30
  339.8 11.7 %custom-call.15 = f32[2,64,64]{2,1,0:T(8,128)S(1)} custom-call(f32[2,64,64]{2,1,0:T(8,128)S(1)} %fusion.128), custom_call_target="Cholesky" | custom-call | tf_op jit(solution)/shard_map/while/body/eval_jaxpr/jit(cholesky)/cholesky | solution.py:14
  351.8 9.8 %custom-call.16 = f32[2,1,64,64]{2,3,1,0:T(8,128)S(1)} custom-call(f32[2,1,64,64]{3,2,1,0:T(8,128)S(1)} %select_bitcast_fusion.3), custom_call_target="InvertDiagBlocksLowerTriangular" | custom-call | tf_op jit(solution)/shard_map/while/body/eval_jaxpr/vmap(jit(_solve_triangular))/triangular_solve | solution.py:16
  382.8 35.3 %all-reduce.7.cloned.1.call-done = f32[2,16,64,64]{3,2,1,0:T(8,128)} async-done(((f32[2,16,64,64]{3,2,1,0:T(8,128)}), f32[2,16,64,64]{3,2,1,0:T(8,128)}) %all-reduce.7.cloned.1.call-update) | async-done | bytes 524304 | tf_op jit(solution)/shard_map/while/body/eval_jaxpr/psum | solution.py:27
  423.9 37.6 %psum.79 = f32[2,64,64]{1,2,0:T(8,128)S(1)} all-reduce(f32[2,64,64]{1,2,0:T(8,128)S(1)} %convolution_bitcast_fusion.10), channel_id=1, replica_groups=mesh['mode'=8,'rep'=4] {'mode'}, use_global_device_ids=true, to_apply=%region_12.14 | all-reduce | flops 8192 | bytes 65536 | tf_op jit(solution)/shard_map/while/body/eval_jaxpr/psum | solution.py:30
  461.6 11.7 %custom-call.15 = f32[2,64,64]{2,1,0:T(8,128)S(1)} custom-call(f32[2,64,64]{2,1,0:T(8,128)S(1)} %fusion.128), custom_call_target="Cholesky" | custom-call | tf_op jit(solution)/shard_map/while/body/eval_jaxpr/jit(cholesky)/cholesky | solution.py:14
  473.5 9.8 %custom-call.16 = f32[2,1,64,64]{2,3,1,0:T(8,128)S(1)} custom-call(f32[2,1,64,64]{3,2,1,0:T(8,128)S(1)} %select_bitcast_fusion.3), custom_call_target="InvertDiagBlocksLowerTriangular" | custom-call | tf_op jit(solution)/shard_map/while/body/eval_jaxpr/vmap(jit(_solve_triangular))/triangular_solve | solution.py:16
  504.5 35.3 %all-reduce.7.cloned.1.call-done = f32[2,16,64,64]{3,2,1,0:T(8,128)} async-done(((f32[2,16,64,64]{3,2,1,0:T(8,128)}), f32[2,16,64,64]{3,2,1,0:T(8,128)}) %all-reduce.7.cloned.1.call-update) | async-done | bytes 524304 | tf_op jit(solution)/shard_map/while/body/eval_jaxpr/psum | solution.py:27
  545.5 37.6 %psum.79 = f32[2,64,64]{1,2,0:T(8,128)S(1)} all-reduce(f32[2,64,64]{1,2,0:T(8,128)S(1)} %convolution_bitcast_fusion.10), channel_id=1, replica_groups=mesh['mode'=8,'rep'=4] {'mode'}, use_global_device_ids=true, to_apply=%region_12.14 | all-reduce | flops 8192 | bytes 65536 | tf_op jit(solution)/shard_map/while/body/eval_jaxpr/psum | solution.py:30
  583.2 11.7 %custom-call.15 = f32[2,64,64]{2,1,0:T(8,128)S(1)} custom-call(f32[2,64,64]{2,1,0:T(8,128)S(1)} %fusion.128), custom_call_target="Cholesky" | custom-call | tf_op jit(solution)/shard_map/while/body/eval_jaxpr/jit(cholesky)/cholesky | solution.py:14
  595.2 9.8 %custom-call.16 = f32[2,1,64,64]{2,3,1,0:T(8,128)S(1)} custom-call(f32[2,1,64,64]{3,2,1,0:T(8,128)S(1)} %select_bitcast_fusion.3), custom_call_target="InvertDiagBlocksLowerTriangular" | custom-call | tf_op jit(solution)/shard_map/while/body/eval_jaxpr/vmap(jit(_solve_triangular))/triangular_solve | solution.py:16
  616.6 10.7 %psum.73 = f32[2,16,64]{2,1,0:T(8,128)} all-reduce(f32[2,16,64]{2,1,0:T(8,128)S(1)} %convolution_bitcast_fusion.4), channel_id=1, replica_groups=mesh['mode'=8,'rep'=4] {'rep'}, use_global_device_ids=true, to_apply=%region_14.17 | all-reduce | flops 2048 | bytes 16384 | tf_op jit(solution)/shard_map/psum | solution.py:85
  (146 shorter events, 111.0 us)
Async XLA Ops:
  7.2 160.1 %copy-start = (f32[2,2,16,64]{3,2,1,0:T(8,128)S(1)}, f32[2,2,16,64]{3,2,1,0:T(8,128)}, u32[]{:S(2)}) copy-start(f32[2,2,16,64]{3,2,1,0:T(8,128)} %param.15) | copy-start | bytes 49156
  7.2 242.3 %all-reduce.5.cloned.1.call-start = ((), (), s32[]{:S(2)}) async-start(), calls=%async_computation | async-start | bytes 262144 | tf_op jit(solution)/shard_map/psum | solution.py:30
  43.9 6.2 copy-start.4
  250.8 365.5 %copy-start.5 = (f32[2,2,16,64]{3,2,1,0:T(8,128)S(1)}, f32[2,2,16,64]{3,2,1,0:T(8,128)}, u32[]{:S(2)}) copy-start(f32[2,2,16,64]{3,2,1,0:T(8,128)} %param.17) | copy-start | bytes 49156
  251.0 5.2 copy-start.2
  251.0 45.4 %all-reduce.7.cloned.1.call-start = ((), (), s32[]{:S(2)}) async-start(), calls=%async_computation.1 | async-start | bytes 2097152 | tf_op jit(solution)/shard_map/while/body/eval_jaxpr/psum | solution.py:27
  260.7 111.0 %all-reduce.9.cloned.1.call-start = ((), (), s32[]{:S(2)}) async-start(), calls=%async_computation.2 | async-start | bytes 262144 | tf_op jit(solution)/shard_map/while/body/eval_jaxpr/psum | solution.py:30
  296.4 3.9 copy-start.1
  363.0 9.9 %copy-start.3 = (f32[4,2,2,64,64]{4,3,2,1,0:T(8,128)S(1)}, f32[4,2,2,64,64]{4,3,2,1,0:T(8,128)}, u32[]{:S(2)}) copy-start(f32[4,2,2,64,64]{4,3,2,1,0:T(8,128)} %copy-done.2) | copy-start | bytes 786436 | tf_op jit(solution)/shard_map/while
  372.9 5.2 copy-start.2
  372.9 45.2 %all-reduce.7.cloned.1.call-start = ((), (), s32[]{:S(2)}) async-start(), calls=%async_computation.1 | async-start | bytes 2097152 | tf_op jit(solution)/shard_map/while/body/eval_jaxpr/psum | solution.py:27
  382.6 110.8 %all-reduce.9.cloned.1.call-start = ((), (), s32[]{:S(2)}) async-start(), calls=%async_computation.2 | async-start | bytes 262144 | tf_op jit(solution)/shard_map/while/body/eval_jaxpr/psum | solution.py:30
  418.1 3.9 copy-start.1
  484.7 9.9 %copy-start.3 = (f32[4,2,2,64,64]{4,3,2,1,0:T(8,128)S(1)}, f32[4,2,2,64,64]{4,3,2,1,0:T(8,128)}, u32[]{:S(2)}) copy-start(f32[4,2,2,64,64]{4,3,2,1,0:T(8,128)} %copy-done.2) | copy-start | bytes 786436 | tf_op jit(solution)/shard_map/while
  494.6 5.2 copy-start.2
  494.6 45.1 %all-reduce.7.cloned.1.call-start = ((), (), s32[]{:S(2)}) async-start(), calls=%async_computation.1 | async-start | bytes 2097152 | tf_op jit(solution)/shard_map/while/body/eval_jaxpr/psum | solution.py:27
  504.3 110.8 %all-reduce.9.cloned.1.call-start = ((), (), s32[]{:S(2)}) async-start(), calls=%async_computation.2 | async-start | bytes 262144 | tf_op jit(solution)/shard_map/while/body/eval_jaxpr/psum | solution.py:30
  539.8 3.9 copy-start.1
  606.4 9.9 %copy-start.3 = (f32[4,2,2,64,64]{4,3,2,1,0:T(8,128)S(1)}, f32[4,2,2,64,64]{4,3,2,1,0:T(8,128)}, u32[]{:S(2)}) copy-start(f32[4,2,2,64,64]{4,3,2,1,0:T(8,128)} %copy-done.2) | copy-start | bytes 786436 | tf_op jit(solution)/shard_map/while
Sparse Core Ops, SparseCore 0:
  178.7 70.7 all-reduce.4
  260.8 35.5 all-reduce.6
  300.4 71.2 all-reduce.8
  382.7 35.3 all-reduce.6
  422.1 71.2 all-reduce.8
  504.4 35.3 all-reduce.6
  543.8 71.2 all-reduce.8
